TPU v7x, 128 devices: a whole 4x4x4 slice. The times are simulated.
128 devices in a mesh: row: 8 (over z_hi, y), col: 16 (over x, z_lo, core).
Axes of the slice: x: 4, y: 4, z: 4 (z_hi: 2, z_lo: 2; z = z_hi * 2 + z_lo), core: 2. Of those that a mesh axis runs over, the one named last changes fastest.
Arguments:
- vectors: bfloat16 [32, 524288], P(None, ('row', 'col')), may hold values from -6 to 6
- tile_values: bfloat16 [81920, 128, 128], P(('row', 'col')), may hold values from -0.0546875 to 0.0546875
- tile_rows: int32 [81920], P(('row', 'col')), may hold values from 0 to 511
- tile_cols: int32 [81920], P(('row', 'col')), may hold values from 0 to 255
- tile_count: int32 [128], P(('row', 'col')), may hold values from 160 to 640, as said below
Outputs:
- filtered: bfloat16 [32, 524288], P(None, ('row', 'col'))
Inputs may be any that keep to these rules, and one draw needn't show every extreme that they name: `tile_count`: every device has at least a quarter of its slots live and some device has all 640 live.
All inputs are finite; a program needn't handle non-finite values.
Results may differ from a plain program's by a relative error of at most 0.014.
Values may be sent and summed in bfloat16 or wider, within the bound.
A program may use at most 128 MiB of HBM per device.

v0:
```python
import jax
import jax.numpy as jnp
from jax import lax
from jax.sharding import PartitionSpec as P


def one_hot_table(indices, count, dtype):
    return (indices[:, None] == jnp.arange(count, dtype=jnp.int32)[None, :]).astype(dtype)


def block_sums(terms, indices, count):
    table = one_hot_table(indices, count, jnp.float32)
    return jnp.einsum("tb,tki->bki", table, terms, precision=lax.Precision.HIGHEST)


def shards(vectors, tile_values, tile_rows, tile_cols, tile_count):
    features = vectors.shape[0]
    own_vertices = vectors.shape[1]
    slot_total = tile_values.shape[0]
    row_gathered = lax.all_gather(vectors, "col", axis=1, tiled=True)
    col_gathered = lax.all_gather(vectors, "row", axis=1, tiled=True)
    row_blocks = row_gathered.shape[1] // 128
    col_blocks = col_gathered.shape[1] // 128
    x_row = row_gathered.reshape(features, row_blocks, 128)
    x_col = col_gathered.reshape(features, col_blocks, 128)
    live_count = tile_count[0]
    alive = (jnp.arange(slot_total, dtype=jnp.int32) < live_count).astype(jnp.float32)
    picked_col = jnp.einsum(
        "tb,kbj->ktj",
        one_hot_table(tile_cols, col_blocks, jnp.bfloat16),
        x_col,
        preferred_element_type=jnp.float32,
    ).astype(jnp.bfloat16)
    picked_row = jnp.einsum(
        "tb,kbi->kti",
        one_hot_table(tile_rows, row_blocks, jnp.bfloat16),
        x_row,
        preferred_element_type=jnp.float32,
    ).astype(jnp.bfloat16)
    to_rows = jnp.einsum(
        "ktj,tij->tki", picked_col, tile_values, preferred_element_type=jnp.float32
    )
    to_cols = jnp.einsum(
        "kti,tij->tkj", picked_row, tile_values, preferred_element_type=jnp.float32
    )
    to_rows, to_cols = (to_rows * alive[:, None, None], to_cols * alive[:, None, None])
    col_sums = block_sums(to_cols, tile_cols, col_blocks)
    row_sums_all = block_sums(to_rows, tile_rows, row_blocks)
    mine_rows = lax.psum_scatter(
        row_sums_all.astype(jnp.bfloat16), "col", scatter_dimension=0, tiled=True
    ).astype(jnp.float32)
    mine_cols = lax.psum_scatter(
        col_sums.astype(jnp.bfloat16), "row", scatter_dimension=0, tiled=True
    ).astype(jnp.float32)
    combined = mine_rows + mine_cols
    return combined.transpose(1, 0, 2).reshape(features, own_vertices).astype(jnp.bfloat16)


def solution(mesh):
    in_specs = (
        P(None, ("row", "col")),
        P(("row", "col"), None, None),
        P(("row", "col")),
        P(("row", "col")),
        P(("row", "col")),
    )
    out_specs = P(None, ("row", "col"))
    return jax.shard_map(shards, mesh=mesh, in_specs=in_specs, out_specs=out_specs, check_vma=False)
```

profile of v0, /device:TPU:0, one launch (start us, length us, event | category | flops | bytes accessed | tf_op | source)
XLA Modules:
  0.0 266.3 jit_solution(13540595652899564749)
XLA Ops:
  6.5 0.0 all-gather.3.cloned.1.call-start
  6.5 0.7 all-gather.3.cloned.1.call-update
  7.3 0.0 all-gather.5.cloned.1.call-start
  7.3 0.7 all-gather.5.cloned.1.call-update
  8.0 0.0 reduce-scatter.3.cloned.1.call-start
  8.7 58.6 %all-gather.3.cloned.1.call-done = bf16[32,32768]{1,0:T(8,128)(2,1)} async-done(((bf16[32,4096]{1,0:T(8,128)(2,1)}), bf16[32,32768]{1,0:T(8,128)(2,1)}) %all-gather.3.cloned.1.call-update) | async-done | bytes 2097168 | tf_op jit(solution)/shard_map/all_gather | solution.py:21
  67.3 2.1 copy.10
  69.4 4.6 %fusion.20 = bf16[640,32,128]{2,0,1:T(8,128)(2,1)} fusion(bf16[32,256,128]{2,1,0:T(8,128)(2,1)S(1)} %bitcast.29, s32[640]{0:T(1024)} %param.8), kind=kOutput, calls=%fused_computation.21 | convolution fusion | flops 1342341120 | bytes 7342592 | tf_op jit(solution)/shard_map/tb,kbj->ktj/dot_general | solution.py:28
  74.0 20.2 %fusion.3 = f32[640,32,128]{2,1,0:T(8,128)} fusion(bf16[640,128,128]{2,1,0:T(8,128)(2,1)} %param.6, bf16[640,32,128]{2,0,1:T(8,128)(2,1)} %fusion.20), kind=kOutput, calls=%fused_computation.7 | convolution fusion | flops 671088640 | bytes 36700160 | tf_op jit(solution)/shard_map/ktj,tij->tki/dot_general | solution.py:40
  94.2 0.0 copy-done.1
  94.2 17.8 %fusion.10 = bf16[512,32,128]{2,0,1:T(8,128)(2,1)} fusion(f32[640,32,128]{2,1,0:T(8,128)} %fusion.3, f32[640]{0:T(1024)S(1)} %fusion.24, s32[640]{0:T(1024)S(1)} %copy-done.1), kind=kOutput, calls=%fused_computation.12 | convolution fusion | flops 16111173632 | bytes 14685184 | tf_op jit(solution)/shard_map/tb,tki->bki/dot_general | solution.py:13
  111.9 0.0 reduce-scatter.3.cloned.1.call-update
  112.0 0.0 reduce-scatter.5.cloned.1.call-start
  112.0 0.0 all-gather.5.cloned.1.call-done
  112.0 3.2 %copy.11 = bf16[4,8,512,128]{3,2,1,0:T(8,128)(2,1)S(1)} copy(bf16[4,8,512,128]{3,1,2,0:T(8,128)(2,1)} %bitcast.30) | data formatting | bytes 8388608
  115.2 4.9 %fusion.13 = bf16[640,32,128]{2,0,1:T(8,128)(2,1)} fusion(bf16[32,512,128]{2,1,0:T(8,128)(2,1)S(1)} %bitcast.31, s32[640]{0:T(1024)S(1)} %copy-done.1), kind=kOutput, calls=%fused_computation.16 | convolution fusion | flops 2684682240 | bytes 9439744 | tf_op jit(solution)/shard_map/tb,kbi->kti/dot_general | solution.py:34
  120.2 17.0 %fusion.6 = f32[640,32,128]{2,1,0:T(8,128)S(1)} fusion(bf16[640,128,128]{2,1,0:T(8,128)(2,1)} %param.6, bf16[640,32,128]{2,0,1:T(8,128)(2,1)} %fusion.13), kind=kOutput, calls=%fused_computation.9 | convolution fusion | flops 671088640 | bytes 36700160 | tf_op jit(solution)/shard_map/kti,tij->tkj/dot_general | solution.py:43
  137.1 0.0 copy-done
  137.1 16.5 %fusion.11 = bf16[256,32,128]{2,0,1:T(8,128)(2,1)} fusion(f32[640,32,128]{2,1,0:T(8,128)S(1)} %fusion.6, f32[640]{0:T(1024)S(1)} %fusion.24, s32[640]{0:T(1024)S(1)} %copy-done), kind=kOutput, calls=%fused_computation.13 | convolution fusion | flops 8056897536 | bytes 12588032 | tf_op jit(solution)/shard_map/tb,tki->bki/dot_general | solution.py:13
  153.7 0.0 reduce-scatter.5.cloned.1.call-update
  153.7 25.0 %reduce-scatter.3.cloned.1.call-done = bf16[32,32,128]{2,0,1:T(8,128)(2,1)} async-done(((bf16[512,32,128]{2,0,1:T(8,128)(2,1)}), bf16[32,32,128]{2,0,1:T(8,128)(2,1)}) %reduce-scatter.3.cloned.1.call-update) | async-done | bytes 262160 | tf_op jit(solution)/shard_map/reduce_scatter | solution.py:49
  178.7 79.1 %reduce-scatter.5.cloned.1.call-done = bf16[32,32,128]{2,0,1:T(8,128)(2,1)} async-done(((bf16[256,32,128]{2,0,1:T(8,128)(2,1)}), bf16[32,32,128]{2,0,1:T(8,128)(2,1)}) %reduce-scatter.5.cloned.1.call-update) | async-done | bytes 262160 | tf_op jit(solution)/shard_map/reduce_scatter | solution.py:52
  257.8 1.1 add_convert_fusion
  258.9 0.8 copy.30
  (3 shorter events, 0.0 us)
Async XLA Ops:
  6.5 60.8 %all-gather.3.cloned.1.call-start = ((), (), s32[]{:S(2)}) async-start(), calls=%async_computation.2 | async-start | bytes 2359296 | tf_op jit(solution)/shard_map/all_gather | solution.py:21
  7.3 104.8 %all-gather.5.cloned.1.call-start = ((), (), s32[]{:S(2)}) async-start(), calls=%async_computation.4 | async-start | bytes 4456448 | tf_op jit(solution)/shard_map/all_gather | solution.py:20
  8.0 170.7 %reduce-scatter.3.cloned.1.call-start = ((), (), s32[]{:S(2)}) async-start(), calls=%async_computation.3 | async-start | bytes 4456448 | tf_op jit(solution)/shard_map/reduce_scatter | solution.py:49
  74.0 20.2 %copy-start.1 = (s32[640]{0:T(1024)S(1)}, s32[640]{0:T(1024)}, u32[]{:S(2)}) copy-start(s32[640]{0:T(1024)} %param.7) | copy-start | bytes 7684
  112.0 145.9 %reduce-scatter.5.cloned.1.call-start = ((), (), s32[]{:S(2)}) async-start(), calls=%async_computation.5 | async-start | bytes 2359296 | tf_op jit(solution)/shard_map/reduce_scatter | solution.py:52
  120.2 17.0 %copy-start = (s32[640]{0:T(1024)S(1)}, s32[640]{0:T(1024)}, u32[]{:S(2)}) copy-start(s32[640]{0:T(1024)} %param.8) | copy-start | bytes 7684
Sparse Core Ops, SparseCore 0:
  9.7 57.5 all-gather.2
  69.0 35.7 all-gather.4
  112.1 66.5 reduce-scatter.2
  182.3 75.4 reduce-scatter.4
where the time goes:
time: 267 us; the launch traced here: 266 us
  waiting for transfers between devices  164 us (61%)
  matrix products  81 us (30%)
  between operations  13.8 us (5%)
  local copies, waits for them, and re-layouts  6.07 us (2%)
    reduce_scatter x1, waiting for transfers between devices, shards(): lax.psum_scatter(col_sums.astype(jnp.bfloat16), 'row', scatter_dimension=...  79.1 us
    all_gather x1, waiting for transfers between devices, shards(): col_gathered = lax.all_gather(vectors, 'row', axis=1, tiled=True)  58.6 us
    dot_general x2, matrix products, block_sums(): jnp.einsum('tb,tki->bki', table, terms, precision=lax.Precision.HIGHEST)  34.3 us
    reduce_scatter x1, waiting for transfers between devices, shards(): lax.psum_scatter(row_sums_all.astype(jnp.bfloat16), 'col', scatter_dimens...  25 us
    dot_general x1, matrix products, shards(): jnp.einsum('ktj,tij->tki', picked_col, tile_values, preferred_element_typ...  20.2 us
    dot_general x1, matrix products, shards(): jnp.einsum('kti,tij->tkj', picked_row, tile_values, preferred_element_typ...  17 us
    unnamed x7, local copies, waits for them, and re-layouts  6.07 us
  transfers between devices with their start and end apart: 4, of which 3 were waited for; matrix products, arithmetic and copies ran while one was open for 32% of the time, Pallas kernels for 0%

commit v1 on v0

--- a/solution.py
+++ b/solution.py
@@ -18,7 +18,9 @@
     own_vertices = vectors.shape[1]
     slot_total = tile_values.shape[0]
     row_gathered = lax.all_gather(vectors, "col", axis=1, tiled=True)
-    col_gathered = lax.all_gather(vectors, "row", axis=1, tiled=True)
+    col_gathered = jnp.concatenate(
+        lax.all_to_all(jnp.stack([vectors] * lax.axis_size("row")), "row", 0, 0), axis=1
+    )
     row_blocks = row_gathered.shape[1] // 128
     col_blocks = col_gathered.shape[1] // 128
     x_row = row_gathered.reshape(features, row_blocks, 128)

time: 267 us -> 253 us (0.948)
  waiting for transfers between devices: 164 us -> 136 us
  starting transfers between devices: 0.12 us -> 7.98 us
  local copies, waits for them, and re-layouts: 6.07 us -> 11.9 us
    all_gather x1 -> x0, waiting for transfers between devices: 58.6 us -> none  [shards(): col_gathered = lax.all_gather(vectors, 'row', axis=1, tiled=True)]
    all_to_all x0 -> x1, waiting for transfers between devices: none -> 29.9 us  [shards(): lax.all_to_all(jnp.stack([vectors] * lax.axis_size('row')), 'row', 0, 0)]
    all_to_all x0 -> x1, starting transfers between devices: none -> 7.89 us  [shards(): lax.all_to_all(jnp.stack([vectors] * lax.axis_size('row')), 'row', 0, 0)]
    another operation x0 -> x2, local copies, waits for them, and re-layouts: none -> 5.43 us  [the longest x1 2.89 us: shards(): x_col = col_gathered.reshape(features, col_blocks, 128)]
    unnamed x7 -> x6, local copies, waits for them, and re-layouts: 6.07 us -> 3.99 us
  transfers between devices with their start and end apart: 4 -> 4, of which waited for: 3 -> 3; matrix products, arithmetic and copies ran while one was open for 32% -> 37% of each run, Pallas kernels for 0% -> 0%
where the time goes in v1:
time: 253 us
  waiting for transfers between devices  136 us (54%)
  matrix products  82.2 us (32%)
  between operations  13.8 us (5%)
  local copies, waits for them, and re-layouts  11.9 us (5%)
  starting transfers between devices  7.98 us (3%)
    reduce_scatter x1, waiting for transfers between devices, shards(): lax.psum_scatter(col_sums.astype(jnp.bfloat16), 'row', scatter_dimension=...  79.2 us
    dot_general x2, matrix products, block_sums(): jnp.einsum('tb,tki->bki', table, terms, precision=lax.Precision.HIGHEST)  34.1 us
    all_to_all x1, waiting for transfers between devices, shards(): lax.all_to_all(jnp.stack([vectors] * lax.axis_size('row')), 'row', 0, 0)  29.9 us
    reduce_scatter x1, waiting for transfers between devices, shards(): lax.psum_scatter(row_sums_all.astype(jnp.bfloat16), 'col', scatter_dimens...  25.7 us
    dot_general x1, matrix products, shards(): jnp.einsum('ktj,tij->tki', picked_col, tile_values, preferred_element_typ...  20.9 us
    dot_general x1, matrix products, shards(): jnp.einsum('kti,tij->tkj', picked_row, tile_values, preferred_element_typ...  18.3 us
    all_to_all x1, starting transfers between devices, shards(): lax.all_to_all(jnp.stack([vectors] * lax.axis_size('row')), 'row', 0, 0)  7.89 us
  transfers between devices with their start and end apart: 4, of which 3 were waited for; matrix products, arithmetic and copies ran while one was open for 37% of the time, Pallas kernels for 0%

profile of v1, /device:TPU:0, one launch (start us, length us, event | category | flops | bytes accessed | tf_op | source)
XLA Modules:
  0.0 252.6 jit_solution(12541569753730291486)
XLA Ops:
  6.5 0.0 all-gather.2.cloned.1.call-start
  6.5 0.7 all-gather.2.cloned.1.call-update
  7.3 2.5 %stack.2 = bf16[8,32,4096]{2,1,0:T(8,128)(2,1)} broadcast(bf16[32,4096]{1,0:T(8,128)(2,1)} %param.5), dimensions={1,2} | broadcast | bytes 2359296 | tf_op jit(solution)/shard_map/stack | solution.py:22
  9.8 7.9 %all-to-all-start = ((bf16[8,32,4096]{2,1,0:T(8,128)(2,1)}), bf16[8,32,4096]{2,1,0:T(8,128)(2,1)S(1)}, u32[]{:S(2)}, u32[]{:S(2)}) async-start(bf16[8,32,4096]{2,1,0:T(8,128)(2,1)} %stack.2), calls=%async_computation | async-start | bytes 4194304 | tf_op jit(solution)/shard_map/all_to_all | solution.py:22
  17.7 0.0 reduce-scatter.3.cloned.1.call-start
  18.4 29.9 %all-to-all-done = bf16[8,32,4096]{2,1,0:T(8,128)(2,1)S(1)} async-done(((bf16[8,32,4096]{2,1,0:T(8,128)(2,1)}), bf16[8,32,4096]{2,1,0:T(8,128)(2,1)S(1)}, u32[]{:S(2)}, u32[]{:S(2)}) %all-to-all-start) | async-done | bytes 2097184 | tf_op jit(solution)/shard_map/all_to_all | solution.py:22
  48.3 2.5 copy.6
  50.8 2.9 %reshape_reshape.3 = bf16[32,256,128]{2,1,0:T(8,128)(2,1)S(1)} reshape(bf16[32,8,4096]{2,1,0:T(8,128)(2,1)} %copy.6) | data formatting | bytes 4194304 | tf_op jit(solution)/shard_map/reshape;reshape | solution.py:27
  53.7 0.0 copy-done
  53.7 3.9 %convert_bitcast_fusion.1 = bf16[32,640,128]{2,1,0:T(8,128)(2,1)} fusion(bf16[32,256,128]{2,1,0:T(8,128)(2,1)S(1)} %reshape_reshape.3, s32[640]{0:T(1024)S(1)} %copy-done), kind=kOutput, calls=%fused_computation.11 | convolution fusion | flops 1344962560 | bytes 7342592 | tf_op jit(solution)/shard_map/tb,kbj->ktj/dot_general | solution.py:30
  57.7 20.9 %broadcast_multiply_fusion.1 = f32[640,32,128]{2,1,0:T(8,128)} fusion(f32[640]{0:T(1024)S(1)} %fusion.28, bf16[640,128,128]{2,1,0:T(8,128)(2,1)} %param.6, bf16[32,640,128]{2,1,0:T(8,128)(2,1)} %convert_bitcast_fusion.1), kind=kOutput, calls=%fused_computation.10 | convolution fusion | flops 673710080 | bytes 36702720 | tf_op jit(solution)/shard_map/ktj,tij->tki/dot_general | solution.py:42
  78.6 17.9 %fusion.12 = bf16[512,32,128]{2,0,1:T(8,128)(2,1)} fusion(f32[640,32,128]{2,1,0:T(8,128)} %broadcast_multiply_fusion.1, s32[640]{0:T(1024)S(1)} %copy-done.1), kind=kOutput, calls=%fused_computation.12 | convolution fusion | flops 16108552192 | bytes 14682624 | tf_op jit(solution)/shard_map/tb,tki->bki/dot_general | solution.py:13
  96.5 0.0 reduce-scatter.3.cloned.1.call-update
  96.5 0.0 reduce-scatter.5.cloned.1.call-start
  96.5 0.0 all-gather.2.cloned.1.call-done
  96.6 3.2 %copy.17 = bf16[4,8,512,128]{3,2,1,0:T(8,128)(2,1)S(1)} copy(bf16[4,8,512,128]{3,1,2,0:T(8,128)(2,1)} %bitcast.29) | data formatting | bytes 8388608
  99.8 5.0 %convert_bitcast_fusion = bf16[32,640,128]{2,1,0:T(8,128)(2,1)} fusion(bf16[32,512,128]{2,1,0:T(8,128)(2,1)S(1)} %bitcast.30, s32[640]{0:T(1024)S(1)} %copy-done.1), kind=kOutput, calls=%fused_computation.8 | convolution fusion | flops 2687303680 | bytes 9439744 | tf_op jit(solution)/shard_map/tb,kbi->kti/dot_general | solution.py:36
  104.8 18.3 %broadcast_multiply_fusion = f32[640,32,128]{2,1,0:T(8,128)S(1)} fusion(f32[640]{0:T(1024)S(1)} %fusion.28, bf16[640,128,128]{2,1,0:T(8,128)(2,1)} %param.6, bf16[32,640,128]{2,1,0:T(8,128)(2,1)} %convert_bitcast_fusion), kind=kOutput, calls=%fused_computation.9 | convolution fusion | flops 673710080 | bytes 36702720 | tf_op jit(solution)/shard_map/kti,tij->tkj/dot_general | solution.py:45
  123.1 16.2 %fusion.15 = bf16[256,32,128]{2,0,1:T(8,128)(2,1)} fusion(f32[640,32,128]{2,1,0:T(8,128)S(1)} %broadcast_multiply_fusion, s32[640]{0:T(1024)S(1)} %copy-done), kind=kOutput, calls=%fused_computation.13 | convolution fusion | flops 8054276096 | bytes 12585472 | tf_op jit(solution)/shard_map/tb,tki->bki/dot_general | solution.py:13
  139.3 0.0 reduce-scatter.5.cloned.1.call-update
  139.3 25.7 %reduce-scatter.3.cloned.1.call-done = bf16[32,32,128]{2,0,1:T(8,128)(2,1)} async-done(((bf16[512,32,128]{2,0,1:T(8,128)(2,1)}), bf16[32,32,128]{2,0,1:T(8,128)(2,1)}) %reduce-scatter.3.cloned.1.call-update) | async-done | bytes 262160 | tf_op jit(solution)/shard_map/reduce_scatter | solution.py:51
  165.0 79.2 %reduce-scatter.5.cloned.1.call-done = bf16[32,32,128]{2,0,1:T(8,128)(2,1)} async-done(((bf16[256,32,128]{2,0,1:T(8,128)(2,1)}), bf16[32,32,128]{2,0,1:T(8,128)(2,1)}) %reduce-scatter.5.cloned.1.call-update) | async-done | bytes 262160 | tf_op jit(solution)/shard_map/reduce_scatter | solution.py:54
  244.2 1.1 add_convert_fusion
  245.3 0.8 copy.36
  (4 shorter events, 0.0 us)
Async XLA Ops:
  6.5 90.0 %all-gather.2.cloned.1.call-start = ((), (), s32[]{:S(2)}) async-start(), calls=%async_computation.4 | async-start | bytes 4456448 | tf_op jit(solution)/shard_map/all_gather | solution.py:20
  9.8 38.5 %all-to-all-start = ((bf16[8,32,4096]{2,1,0:T(8,128)(2,1)}), bf16[8,32,4096]{2,1,0:T(8,128)(2,1)S(1)}, u32[]{:S(2)}, u32[]{:S(2)}) async-start(bf16[8,32,4096]{2,1,0:T(8,128)(2,1)} %stack.2), calls=%async_computation | async-start | bytes 4194304 | tf_op jit(solution)/shard_map/all_to_all | solution.py:22
  17.7 36.0 %copy-start = (s32[640]{0:T(1024)S(1)}, s32[640]{0:T(1024)}, u32[]{:S(2)}) copy-start(s32[640]{0:T(1024)} %param.8) | copy-start | bytes 7684
  17.7 147.3 %reduce-scatter.3.cloned.1.call-start = ((), (), s32[]{:S(2)}) async-start(), calls=%async_computation.3 | async-start | bytes 4456448 | tf_op jit(solution)/shard_map/reduce_scatter | solution.py:51
  57.7 20.9 %copy-start.1 = (s32[640]{0:T(1024)S(1)}, s32[640]{0:T(1024)}, u32[]{:S(2)}) copy-start(s32[640]{0:T(1024)} %param.7) | copy-start | bytes 7684
  96.5 147.7 %reduce-scatter.5.cloned.1.call-start = ((), (), s32[]{:S(2)}) async-start(), calls=%async_computation.5 | async-start | bytes 2359296 | tf_op jit(solution)/shard_map/reduce_scatter | solution.py:54
Sparse Core Ops, SparseCore 0:
  9.0 57.9 all-gather.1
  96.6 68.3 reduce-scatter.2
  168.8 75.3 reduce-scatter.4
